TPU v7x, 32 devices: a whole 2x2x4 slice. The times are simulated.
32 devices in a mesh: dp: 4 (over y, core), ctx: 2 (over x), tensor: 4 (over z).
Axes of the slice: x: 2, y: 2, z: 4, core: 2. Of those that a mesh axis runs over, the one named last changes fastest.
Arguments:
- layer_input: bfloat16 [4, 512, 8192], P('dp', ('ctx', 'tensor')), may hold values from -6 to 6
- queries: bfloat16 [4, 512, 8192], P('dp', 'ctx', 'tensor'), may hold values from -12 to 12
- forward_output: bfloat16 [4, 512, 8192], P('dp', 'ctx', 'tensor'), may hold values from -6 to 6
- attention_output_gradient: bfloat16 [4, 512, 8192], P('dp', 'ctx', 'tensor'), may hold values from -6 to 6
- key_weight: bfloat16 [8192, 1024], P(None, 'tensor'), may hold values from -3 to 3
- value_projection_weight: bfloat16 [8192, 1024], P(None, 'tensor'), may hold values from -0.0625 to 0.0625
- segment: int32 [4, 512], P('dp'), may hold values from 0 to 4, as said below
- block_table: int32 [4, 4, 4], P('dp'), may hold values from 0 to 1, as said below
- block_owner: int32 [4, 4], P('dp'), may hold values from 0 to 3, each once within a row
Outputs:
- query_grad: bfloat16 [4, 512, 8192], P('dp', 'ctx', 'tensor')
- input_grad: bfloat16 [4, 512, 8192], P('dp', ('ctx', 'tensor'))
- key_weight_grad: bfloat16 [8192, 1024], P(('dp', 'ctx'), 'tensor')
- value_weight_grad: bfloat16 [8192, 1024], P(('dp', 'ctx'), 'tensor')
Inputs may be any that keep to these rules, and one draw needn't show every extreme that they name: Along the logical positions of a group the segment never falls; the prompt (0) comes first and every rollout 1 to 4 is present. block_table[g, b, c] is 1 only where some position of logical block b may read some position of logical block c under the causal and segment rule; block_table[g, b, b] is 1 for every block; other such pairs may be 0. `block_owner`: each group's row holds every logical block once.
All inputs are finite; a program needn't handle non-finite values.
Results may differ from a plain program's by a relative error of at most 0.005.
The roundings to bfloat16 on the way count: a program that leaves them out, or rounds other values in their place, can miss the bound.
Values may be sent and summed in bfloat16 or wider, within the bound.
A program may use at most 128 MiB of HBM per device.

v0:
```python
import math
import jax
import jax.numpy as jnp
from jax import lax
from jax.sharding import PartitionSpec as P

HEAD_SIZE = 128
BLK = 128


def per_device(
    layer_input,
    queries,
    forward_output,
    attention_output_gradient,
    key_weight,
    value_projection_weight,
    segment,
    block_table,
    block_owner,
):
    softmax_scale = 1.0 / math.sqrt(HEAD_SIZE)
    local_rows = queries.shape[1]
    kv_local = key_weight.shape[1] // HEAD_SIZE
    q_local = queries.shape[2] // HEAD_SIZE
    queries_per_group = q_local // kv_local
    kv_width = kv_local * HEAD_SIZE
    gathered = lax.all_gather(layer_input, "tensor", axis=1, tiled=True)[0]
    planes = lax.axis_size("tensor")
    plane_size = lax.axis_size("dp") * lax.axis_size("ctx")
    plane_index = lax.axis_index("dp") * lax.axis_size("ctx") + lax.axis_index("ctx")
    model_width = key_weight.shape[0]
    piece_rows = model_width // (planes * plane_size)

    def piece(weight):
        split = weight.reshape(planes, plane_size, piece_rows, kv_width)
        return lax.dynamic_index_in_dim(split, plane_index, 1, keepdims=False)

    pieces = jnp.concatenate([piece(key_weight), piece(value_projection_weight)], axis=2)
    pieces = lax.all_to_all(pieces, "tensor", split_axis=0, concat_axis=0, tiled=True)
    wide_weight = lax.all_gather(pieces, ("dp", "ctx"), axis=1, tiled=True)
    plane_input = lax.all_to_all(gathered, ("dp", "ctx"), split_axis=1, concat_axis=0, tiled=True)
    projected_keys = jnp.dot(gathered, key_weight, preferred_element_type=jnp.float32)
    projected_values = jnp.dot(
        gathered, value_projection_weight, preferred_element_type=jnp.float32
    )
    kv_rows = jnp.concatenate([projected_keys, projected_values], axis=1).astype(jnp.bfloat16)
    owner_row = block_owner[0]
    segments_row = segment[0]
    table_row = block_table[0]
    blocks_here = local_rows // BLK
    ctx_index = lax.axis_index("ctx")
    own_blocks = lax.dynamic_slice_in_dim(owner_row, ctx_index * blocks_here, blocks_here)
    offsets = jnp.arange(BLK, dtype=jnp.int32)
    query_pos = (own_blocks[:, None] * BLK + offsets[None, :]).reshape(-1)
    query_seg = jnp.take(segments_row, query_pos)
    own_table = jnp.take(table_row, own_blocks, axis=0)
    query_heads = queries[0].reshape(local_rows, kv_local, queries_per_group, HEAD_SIZE)
    grad_heads = attention_output_gradient[0].reshape(
        local_rows, kv_local, queries_per_group, HEAD_SIZE
    )
    saved_heads = forward_output[0].reshape(local_rows, kv_local, queries_per_group, HEAD_SIZE)
    correction = jnp.sum(grad_heads.astype(jnp.float32) * saved_heads.astype(jnp.float32), axis=-1)
    correction = correction.transpose(1, 2, 0)

    def allowed_for(leading_row, row_count):
        key_blocks = lax.dynamic_slice_in_dim(owner_row, leading_row // BLK, row_count // BLK)
        key_pos = (key_blocks[:, None] * BLK + offsets[None, :]).reshape(-1)
        key_seg = jnp.take(segments_row, key_pos)
        table_part = jnp.take(own_table, key_blocks, axis=1) == 1
        table_full = jnp.broadcast_to(
            table_part[:, None, :, None], (blocks_here, BLK, row_count // BLK, BLK)
        )
        table_full = table_full.reshape(local_rows, row_count)
        same_tree = (key_seg[None, :] == 0) | (key_seg[None, :] == query_seg[:, None])
        return table_full & (key_pos[None, :] <= query_pos[:, None]) & same_tree

    def block_scores(block_rows, leading_row):
        row_count = block_rows.shape[0]
        block_keys = block_rows[:, :kv_width].reshape(row_count, kv_local, HEAD_SIZE)
        block_values = block_rows[:, kv_width:].reshape(row_count, kv_local, HEAD_SIZE)
        raw_scores = (
            jnp.einsum(
                "qhgd,khd->hgqk", query_heads, block_keys, preferred_element_type=jnp.float32
            )
            * softmax_scale
        )
        allowed = allowed_for(leading_row, row_count)
        return (jnp.where(allowed[None, None], raw_scores, -jnp.inf), block_keys, block_values)

    def stats_block(carried, block_rows, leading_row):
        running_max, running_sum = carried
        scores = block_scores(block_rows, leading_row)[0]
        new_max = jnp.maximum(running_max, jnp.max(scores, axis=-1))
        running_sum = running_sum * jnp.exp(running_max - new_max) + jnp.sum(
            jnp.exp(scores - new_max[..., None]), axis=-1
        )
        return (new_max, running_sum)

    def grads_block(carried, block_rows, leading_row, log_norm):
        query_sum, keyval_sum = carried
        row_count = block_rows.shape[0]
        scores, block_keys, block_values = block_scores(block_rows, leading_row)
        probabilities = jnp.exp(scores - log_norm[..., None])
        probs_low = probabilities.astype(jnp.bfloat16)
        value_gradient_rows = jnp.einsum(
            "hgqk,qhgd->khd", probs_low, grad_heads, preferred_element_type=jnp.float32
        )
        prob_grads = jnp.einsum(
            "qhgd,khd->hgqk", grad_heads, block_values, preferred_element_type=jnp.float32
        )
        score_low = (probabilities * (prob_grads - correction[..., None])).astype(jnp.bfloat16)
        query_sum = query_sum + jnp.einsum(
            "hgqk,khd->qhgd", score_low, block_keys, preferred_element_type=jnp.float32
        )
        key_gradient_rows = (
            jnp.einsum("hgqk,qhgd->khd", score_low, query_heads, preferred_element_type=jnp.float32)
            * softmax_scale
        )
        update = jnp.concatenate(
            [
                key_gradient_rows.reshape(row_count, kv_width),
                value_gradient_rows.reshape(row_count, kv_width),
            ],
            axis=1,
        )
        keyval_sum = lax.dynamic_update_slice_in_dim(keyval_sum, update, leading_row, 0)
        return (query_sum, keyval_sum)

    def over_blocks(block_step, carried, shard_part):
        row_count = shard_part.shape[0]
        block_size = math.gcd(row_count, max(512, local_rows))
        block_count = row_count // block_size
        pieces = shard_part.reshape(block_count, block_size, shard_part.shape[1])
        starts = block_size * jnp.arange(block_count, dtype=jnp.int32)

        def one_block(state_in, scan_item):
            block_rows, block_start = scan_item
            result = block_step(state_in, block_rows, block_start)
            return (result, None)

        carried, _ = lax.scan(one_block, carried, (pieces, starts))
        return carried

    stats_init = (
        jnp.full((kv_local, queries_per_group, local_rows), -1e30, jnp.float32),
        jnp.zeros((kv_local, queries_per_group, local_rows), jnp.float32),
    )
    seq_rows = local_rows * lax.axis_size("ctx")
    grads_init = (
        jnp.zeros((local_rows, kv_local, queries_per_group, HEAD_SIZE), jnp.float32),
        jnp.zeros((seq_rows, 2 * kv_width), jnp.float32),
    )
    running_max, running_sum = over_blocks(
        stats_block, stats_init, lax.all_gather(kv_rows, "ctx", axis=0, tiled=True)
    )
    log_norm = running_max + jnp.log(running_sum)

    def grads_fold(carried, shard_part):
        return over_blocks(
            lambda state, rows_in, start_in: grads_block(state, rows_in, start_in, log_norm),
            carried,
            shard_part,
        )

    query_sum, keyval_sum = grads_fold(
        grads_init, lax.all_gather(kv_rows, "ctx", axis=0, tiled=True)
    )
    own_grads = lax.psum_scatter(keyval_sum, "ctx", scatter_dimension=0, tiled=True).astype(
        jnp.bfloat16
    )
    query_grad = (
        (query_sum * softmax_scale).astype(jnp.bfloat16).reshape(1, local_rows, q_local * HEAD_SIZE)
    )
    kv_all = lax.all_gather(own_grads, "tensor", axis=0)
    kv_plane = lax.all_gather(own_grads, ("dp", "ctx"), axis=0, tiled=True)
    width_part = lax.dot_general(
        kv_all, wide_weight, (((0, 2), (0, 2)), ((), ())), preferred_element_type=jnp.float32
    ).astype(jnp.bfloat16)
    input_grad = lax.all_to_all(width_part, "tensor", split_axis=0, concat_axis=1, tiled=True)[None]
    weight_sum = lax.dot_general(
        plane_input, kv_plane, (((0,), (0,)), ((), ())), preferred_element_type=jnp.float32
    )
    key_weight_grad = weight_sum[:, :kv_width].astype(jnp.bfloat16)
    value_weight_grad = weight_sum[:, kv_width:].astype(jnp.bfloat16)
    return (query_grad, input_grad, key_weight_grad, value_weight_grad)


def solution(mesh):
    in_specs = (
        P("dp", ("ctx", "tensor"), None),
        P("dp", "ctx", "tensor"),
        P("dp", "ctx", "tensor"),
        P("dp", "ctx", "tensor"),
        P(None, "tensor"),
        P(None, "tensor"),
        P("dp", None),
        P("dp", None, None),
        P("dp", None),
    )
    out_specs = (
        P("dp", "ctx", "tensor"),
        P("dp", ("ctx", "tensor"), None),
        P(("dp", "ctx"), "tensor"),
        P(("dp", "ctx"), "tensor"),
    )
    return jax.shard_map(
        per_device, mesh=mesh, in_specs=in_specs, out_specs=out_specs, check_vma=False
    )
```

profile of v0, /device:TPU:0, one launch (start us, length us, event | category | flops | bytes accessed | tf_op | source)
XLA Modules:
  0.0 300.7 jit_solution(7361246667366215008)
XLA Ops:
  7.2 0.7 all-gather.6.cloned.1.call-update
  8.0 0.7 fusion.21
  8.7 1.2 gather_fusion
  10.0 0.7 compare_and_fusion.1
  10.7 0.1 broadcast_select_fusion
  10.8 0.1 copy.70
  10.9 0.7 bitcast_multiply_fusion.1
  11.5 0.6 gather_fusion.2
  12.1 0.7 compare_and_fusion
  12.8 0.1 bitcast_compare_fusion
  12.8 0.1 copy.71
  12.9 0.7 bitcast_multiply_fusion
  13.7 0.1 fusion.24
  13.8 1.9 gather_fusion.1
  15.7 0.1 compare_select_fusion.1
  15.8 3.5 %gather_fusion.3 = s32[512]{0:T(512)S(1)} fusion(s32[512]{0:T(512)S(1)} %bitcast.138, s32[1024]{0:T(1024)S(1)} %pad_clamp_fusion.1), kind=kCustom, calls=%fused_computation.1.clone | custom fusion | bytes 6144 | tf_op jit(solution)/shard_map/while/body/eval_jaxpr/jit(_take)/gather | solution.py:69
  19.4 0.1 and_select_fusion.1
  19.5 0.1 broadcast_compare_fusion
  19.6 0.1 broadcast_in_dim.108
  19.7 0.2 fusion.20
  19.9 0.3 copy.72
  20.2 0.5 copy.106
  20.8 1.5 copy.108
  22.2 1.6 copy.82
  23.8 0.2 convert_bitcast_fusion
  24.0 0.4 copy.109
  24.4 0.9 multiply_reduce_fusion
  25.3 0.1 copy.77
  25.4 67.6 %all-gather.6.cloned.1.call-done = bf16[1,256,8192]{2,1,0:T(8,128)(2,1)} async-done(((bf16[1,64,8192]{2,1,0:T(8,128)(2,1)}), bf16[1,256,8192]{2,1,0:T(8,128)(2,1)}) %all-gather.6.cloned.1.call-update) | async-done | bytes 4194320 | tf_op jit(solution)/shard_map/all_gather | solution.py:28
  93.1 5.3 %fusion.14 = bf16[256,256]{0,1:T(8,128)(2,1)S(1)} fusion(bf16[8192,256]{1,0:T(8,128)(2,1)} %param.17, bf16[1,256,8192]{2,1,0:T(8,128)(2,1)} %all-gather.6.cloned.1.call-done), kind=kOutput, calls=%fused_computation.27 | convolution fusion | flops 1073807360 | bytes 8519680 | tf_op jit(solution)/shard_map/dot_general | solution.py:43
  98.4 0.6 copy-done.4
  99.0 1.9 fusion.17
  100.9 8.9 %all_gather.20 = bf16[512,512]{0,1:T(8,128)(2,1)S(1)} all-gather(bf16[256,512]{0,1:T(8,128)(2,1)S(1)} %pad_maximum_fusion.2), channel_id=1, replica_groups=mesh['dp'=4,'ctx'=2,'tensor'=4] {'ctx'}, dimensions={0}, use_global_device_ids=true | all-gather | bytes 786432 | tf_op jit(solution)/shard_map/all_gather | solution.py:167
  109.9 1.4 fusion.3
  111.3 1.7 exponential_reduce_fusion
  113.0 2.3 fusion.8
  115.3 2.9 fusion.1
  118.2 2.0 copy-done.3
  120.2 1.5 fusion.13
  121.7 1.0 pad_maximum_fusion
  122.7 1.3 dynamic-slice_bitcast_fusion
  124.0 1.1 pad_maximum_fusion.1
  125.1 3.6 %all-to-all-start = ((bf16[4,256,512]{2,1,0:T(8,128)(2,1)}), bf16[4,256,512]{2,1,0:T(8,128)(2,1)S(1)}, u32[]{:S(2)}, u32[]{:S(2)}) async-start(bf16[4,256,512]{2,1,0:T(8,128)(2,1)} %pad_maximum_fusion.1), calls=%async_computation.1 | async-start | bytes 2097152 | tf_op jit(solution)/shard_map/all_to_all | solution.py:40
  128.7 13.1 %reduce-scatter.2.cloned.1.call-done = f32[256,512]{0,1:T(8,128)} async-done(((f32[512,512]{0,1:T(8,128)}), f32[256,512]{0,1:T(8,128)}) %reduce-scatter.2.cloned.1.call-update) | async-done | bytes 524304 | tf_op jit(solution)/shard_map/reduce_scatter | solution.py:169
  141.8 1.8 convert_element_type.47
  143.7 10.1 %all-to-all-done = bf16[4,256,512]{2,1,0:T(8,128)(2,1)S(1)} async-done(((bf16[4,256,512]{2,1,0:T(8,128)(2,1)}), bf16[4,256,512]{2,1,0:T(8,128)(2,1)S(1)}, u32[]{:S(2)}, u32[]{:S(2)}) %all-to-all-start) | async-done | bytes 1048608 | tf_op jit(solution)/shard_map/all_to_all | solution.py:40
  153.7 1.0 copy-done.5
  154.7 6.4 %copy.87 = bf16[1,256,8192]{1,2,0:T(8,128)(2,1)} copy(bf16[1,256,8192]{2,1,0:T(8,128)(2,1)} %all-gather.6.cloned.1.call-done) | data formatting | bytes 8388608 | tf_op jit(solution)/shard_map/all_gather | solution.py:28
  161.1 4.6 %all-to-all-start.2 = ((bf16[256,8,1024]{0,2,1:T(8,128)(2,1)}), bf16[256,8,1024]{0,2,1:T(8,128)(2,1)}, u32[]{:S(2)}, u32[]{:S(2)}) async-start(bf16[256,8,1024]{0,2,1:T(8,128)(2,1)} %bitcast.140), calls=%async_computation.3 | async-start | bytes 8388608 | tf_op jit(solution)/shard_map/all_to_all | solution.py:42
  165.7 0.5 all-gather.10.cloned.1.call-update
  166.3 8.0 %all-gather.12.cloned.1.call-done = bf16[1024,512]{0,1:T(8,128)(2,1)} async-done(((bf16[256,512]{0,1:T(8,128)(2,1)}), bf16[1024,512]{0,1:T(8,128)(2,1)}) %all-gather.12.cloned.1.call-update) | async-done | bytes 1048592 | tf_op jit(solution)/shard_map/all_gather | solution.py:175
  174.3 1.5 copy.83
  175.8 78.1 %all-gather.8.cloned.1.call-done = bf16[4,2048,512]{2,1,0:T(8,128)(2,1)} async-done(((bf16[4,256,512]{2,1,0:T(8,128)(2,1)}), bf16[4,2048,512]{2,1,0:T(8,128)(2,1)}) %all-gather.8.cloned.1.call-update) | async-done | bytes 8388624 | tf_op jit(solution)/shard_map/all_gather | solution.py:41
  253.9 6.7 %fusion.11 = bf16[256,2048]{1,0:T(8,128)(2,1)} fusion(bf16[4,256,512]{2,1,0:T(8,128)(2,1)S(1)} %bitcast.155, bf16[4,2048,512]{2,1,0:T(8,128)(2,1)} %all-gather.8.cloned.1.call-done), kind=kOutput, calls=%fused_computation.19 | convolution fusion | flops 2148007936 | bytes 10485760 | tf_op jit(solution)/shard_map/dot_general | solution.py:177
  260.6 4.6 %all-to-all-start.1 = ((bf16[4,64,2048]{2,1,0:T(8,128)(2,1)}), bf16[4,64,2048]{2,1,0:T(8,128)(2,1)S(1)}, u32[]{:S(2)}, u32[]{:S(2)}) async-start(bf16[4,64,2048]{2,1,0:T(8,128)(2,1)} %bitcast.37), calls=%async_computation.2 | async-start | bytes 2097152 | tf_op jit(solution)/shard_map/all_to_all | solution.py:180
  265.2 2.9 multiply_convert_fusion
  268.1 1.4 copy.89
  269.5 6.4 %copy.88 = bf16[8,256,1024]{2,1,0:T(8,128)(2,1)} copy(bf16[8,256,1024]{1,2,0:T(8,128)(2,1)} %bitcast.40) | data formatting | bytes 8388608 | tf_op jit(solution)/shard_map/all_to_all | solution.py:42
  276.0 8.6 %all-gather.10.cloned.1.call-done = bf16[2048,512]{0,1:T(8,128)(2,1)} async-done(((bf16[256,512]{0,1:T(8,128)(2,1)}), bf16[2048,512]{0,1:T(8,128)(2,1)}) %all-gather.10.cloned.1.call-update) | async-done | bytes 2097168 | tf_op jit(solution)/shard_map/all_gather | solution.py:176
  284.6 5.2 %fusion.12 = bf16[1024,512]{0,1:T(8,128)(2,1)S(1)} fusion(bf16[2048,512]{0,1:T(8,128)(2,1)} %all-gather.10.cloned.1.call-done, bf16[2048,1024]{1,0:T(8,128)(2,1)} %bitcast.148), kind=kOutput, calls=%fused_computation.24 | convolution fusion | flops 2148007936 | bytes 7340032 | tf_op jit(solution)/shard_map/dot_general | solution.py:181
  289.8 1.0 copy.90
  290.8 1.0 copy.91
  291.8 0.8 copy.86
  292.6 1.6 broadcast_in_dim.114
  (36 shorter events, 0.6 us)
Async XLA Ops:
  7.2 6.6 %copy-start = (s32[1,512]{1,0:T(1,128)S(1)}, s32[1,512]{1,0:T(1,128)}, u32[]{:S(2)}) copy-start(s32[1,512]{1,0:T(1,128)} %param.19) | copy-start | bytes 6148
  7.2 13.0 %copy-start.7 = (bf16[1,256,2048]{2,1,0:T(8,128)(2,1)S(1)}, bf16[1,256,2048]{2,1,0:T(8,128)(2,1)}, u32[]{:S(2)}) copy-start(bf16[1,256,2048]{2,1,0:T(8,128)(2,1)} %param.14) | copy-start | bytes 3145732
  7.2 85.9 %all-gather.6.cloned.1.call-start = ((), (), s32[]{:S(2)}) async-start(), calls=%async_computation.4 | async-start | bytes 5242880 | tf_op jit(solution)/shard_map/all_gather | solution.py:28
  7.9 133.9 %reduce-scatter.2.cloned.1.call-start = ((), (), s32[]{:S(2)}) async-start(), calls=%async_computation.5 | async-start | bytes 1572864 | tf_op jit(solution)/shard_map/reduce_scatter | solution.py:169
  15.8 8.0 %copy-start.6 = (bf16[1,256,2048]{2,1,0:T(8,128)(2,1)S(1)}, bf16[1,256,2048]{2,1,0:T(8,128)(2,1)}, u32[]{:S(2)}) copy-start(bf16[1,256,2048]{2,1,0:T(8,128)(2,1)} %param.15) | copy-start | bytes 3145732
  93.1 5.3 %copy-start.2 = (bf16[1,256,8192]{2,1,0:T(8,128)(2,1)S(1)}, bf16[1,256,8192]{2,1,0:T(8,128)(2,1)}, u32[]{:S(2)}) copy-start(bf16[1,256,8192]{2,1,0:T(8,128)(2,1)} %all-gather.6.cloned.1.call-done) | copy-start | bytes 12582916
  93.1 5.9 %copy-start.4 = (bf16[8192,256]{1,0:T(8,128)(2,1)S(1)}, bf16[8192,256]{1,0:T(8,128)(2,1)}, u32[]{:S(2)}) copy-start(bf16[8192,256]{1,0:T(8,128)(2,1)} %param.18) | copy-start | bytes 12582916
  111.3 1.8 copy-start.8
  118.2 2.0 copy-start.3
  125.1 28.6 %all-to-all-start = ((bf16[4,256,512]{2,1,0:T(8,128)(2,1)}), bf16[4,256,512]{2,1,0:T(8,128)(2,1)S(1)}, u32[]{:S(2)}, u32[]{:S(2)}) async-start(bf16[4,256,512]{2,1,0:T(8,128)(2,1)} %pad_maximum_fusion.1), calls=%async_computation.1 | async-start | bytes 2097152 | tf_op jit(solution)/shard_map/all_to_all | solution.py:40
  128.7 45.6 %all-gather.12.cloned.1.call-start = ((), (), s32[]{:S(2)}) async-start(), calls=%async_computation.8 | async-start | bytes 1310720 | tf_op jit(solution)/shard_map/all_gather | solution.py:175
  143.6 110.3 %all-gather.8.cloned.1.call-start = ((), (), s32[]{:S(2)}) async-start(), calls=%async_computation.6 | async-start | bytes 9437184 | tf_op jit(solution)/shard_map/all_gather | solution.py:41
  153.7 1.0 copy-start.5
  161.1 99.5 %all-to-all-start.2 = ((bf16[256,8,1024]{0,2,1:T(8,128)(2,1)}), bf16[256,8,1024]{0,2,1:T(8,128)(2,1)}, u32[]{:S(2)}, u32[]{:S(2)}) async-start(bf16[256,8,1024]{0,2,1:T(8,128)(2,1)} %bitcast.140), calls=%async_computation.3 | async-start | bytes 8388608 | tf_op jit(solution)/shard_map/all_to_all | solution.py:42
  165.7 118.9 %all-gather.10.cloned.1.call-start = ((), (), s32[]{:S(2)}) async-start(), calls=%async_computation.7 | async-start | bytes 2359296 | tf_op jit(solution)/shard_map/all_gather | solution.py:176
  260.6 31.2 %all-to-all-start.1 = ((bf16[4,64,2048]{2,1,0:T(8,128)(2,1)}), bf16[4,64,2048]{2,1,0:T(8,128)(2,1)S(1)}, u32[]{:S(2)}, u32[]{:S(2)}) async-start(bf16[4,64,2048]{2,1,0:T(8,128)(2,1)} %bitcast.37), calls=%async_computation.2 | async-start | bytes 2097152 | tf_op jit(solution)/shard_map/all_to_all | solution.py:180
  284.6 9.7 %copy-start.1 = (s32[1,512]{1,0:T(1,128)S(1)}, s32[1,512]{1,0:T(1,128)}, u32[]{:S(2)}) copy-start(s32[1,512]{1,0:T(1,128)} %param.19) | copy-start | bytes 6148
Sparse Core Ops, SparseCore 0:
  9.6 83.4 all-gather.5
  122.9 18.9 reduce-scatter.1
  144.0 30.2 all-gather.11
  176.8 77.0 all-gather.7
  256.3 28.1 all-gather.9
where the time goes:
time: 302 us; the launch traced here: 301 us
  waiting for transfers between devices  187 us (62%)
  local copies, waits for them, and re-layouts  37 us (12%)
  matrix products  30 us (10%)
  between operations  14.1 us (5%)
  starting transfers between devices  13 us (4%)
  other arithmetic  11.1 us (4%)
  blocking collectives  8.92 us (3%)
    all_gather x1, waiting for transfers between devices, per_device(): wide_weight = lax.all_gather(pieces, ('dp', 'ctx'), axis=1, tiled=True)  78.1 us
    all_gather x1, waiting for transfers between devices, per_device(): gathered = lax.all_gather(layer_input, 'tensor', axis=1, tiled=True)[0]  67.6 us
    reduce_scatter x1, waiting for transfers between devices, per_device(): lax.psum_scatter(keyval_sum, 'ctx', scatter_dimension=0, tiled=True)  13.1 us
    all_to_all x1, waiting for transfers between devices, per_device(): lax.all_to_all(pieces, 'tensor', split_axis=0, concat_axis=0, tiled=True)  10.1 us
    all_gather x1, blocking collectives, per_device(): lax.all_gather(kv_rows, 'ctx', axis=0, tiled=True)  8.92 us
    unnamed x23, local copies, waits for them, and re-layouts  8.82 us
    all_gather x1, waiting for transfers between devices, per_device(): kv_plane = lax.all_gather(own_grads, ('dp', 'ctx'), axis=0, tiled=True)  8.59 us
    all_gather x1, waiting for transfers between devices, per_device(): kv_all = lax.all_gather(own_grads, 'tensor', axis=0)  7.99 us
  transfers between devices with their start and end apart: 8, of which 6 were waited for; matrix products, arithmetic and copies ran while one was open for 18% of the time, Pallas kernels for 0%

commit v1 on v0

--- a/solution.py
+++ b/solution.py
@@ -39,7 +39,9 @@
     pieces = jnp.concatenate([piece(key_weight), piece(value_projection_weight)], axis=2)
     pieces = lax.all_to_all(pieces, "tensor", split_axis=0, concat_axis=0, tiled=True)
     wide_weight = lax.all_gather(pieces, ("dp", "ctx"), axis=1, tiled=True)
-    plane_input = lax.all_to_all(gathered, ("dp", "ctx"), split_axis=1, concat_axis=0, tiled=True)
+    parts = jnp.split(gathered, lax.axis_size(("dp", "ctx")), axis=1)
+    arrived = lax.all_to_all(jnp.stack(parts), ("dp", "ctx"), 0, 0)
+    plane_input = jnp.concatenate(arrived, axis=0)
     projected_keys = jnp.dot(gathered, key_weight, preferred_element_type=jnp.float32)
     projected_values = jnp.dot(
         gathered, value_projection_weight, preferred_element_type=jnp.float32

time: 302 us -> 306 us (1.013)
  waiting for transfers between devices: 187 us -> 194 us
    unnamed x23 -> x30, local copies, waits for them, and re-layouts: 8.82 us -> 17.1 us
    all_gather x1, waiting for transfers between devices: 8.59 us -> 15 us  [per_device(): kv_plane = lax.all_gather(own_grads, ('dp', 'ctx'), axis=0, tiled=True)]
    all_to_all x1 -> x0, local copies, waits for them, and re-layouts: 6.44 us -> none  [per_device(): lax.all_to_all(gathered, ('dp', 'ctx'), split_axis=1, concat_axis=0, tile...]
    all_gather x1 -> x0, local copies, waits for them, and re-layouts: 6.36 us -> none  [per_device(): gathered = lax.all_gather(layer_input, 'tensor', axis=1, tiled=True)[0]]
    all_gather x1, waiting for transfers between devices: 78.1 us -> 82.8 us  [per_device(): wide_weight = lax.all_gather(pieces, ('dp', 'ctx'), axis=1, tiled=True)]
    all_gather x1, waiting for transfers between devices: 7.99 us -> 3.26 us  [per_device(): kv_all = lax.all_gather(own_grads, 'tensor', axis=0)]
    dot_general x1, matrix products: 5.33 us -> 1.86 us  [per_device(): jnp.dot(gathered, key_weight, preferred_element_type=jnp.float32)]
    dot_general x1, matrix products: 1.86 us -> 5.33 us  [per_device(): jnp.dot(gathered, value_projection_weight, preferred_element_type=jnp.flo...]
  transfers between devices with their start and end apart: 8 -> 8, of which waited for: 6 -> 7; matrix products, arithmetic and copies ran while one was open for 18% -> 17% of each run, Pallas kernels for 0% -> 0%
where the time goes in v1:
time: 306 us; the launch traced here: 305 us
  waiting for transfers between devices  194 us (63%)
  local copies, waits for them, and re-layouts  34.2 us (11%)
  matrix products  30.1 us (10%)
  between operations  14.1 us (5%)
  starting transfers between devices  13 us (4%)
  other arithmetic  11.1 us (4%)
  blocking collectives  8.92 us (3%)
    all_gather x1, waiting for transfers between devices, per_device(): wide_weight = lax.all_gather(pieces, ('dp', 'ctx'), axis=1, tiled=True)  82.8 us
    all_gather x1, waiting for transfers between devices, per_device(): gathered = lax.all_gather(layer_input, 'tensor', axis=1, tiled=True)[0]  67.7 us
    unnamed x30, local copies, waits for them, and re-layouts  17.1 us
    all_gather x1, waiting for transfers between devices, per_device(): kv_plane = lax.all_gather(own_grads, ('dp', 'ctx'), axis=0, tiled=True)  15 us
    reduce_scatter x1, waiting for transfers between devices, per_device(): lax.psum_scatter(keyval_sum, 'ctx', scatter_dimension=0, tiled=True)  13.1 us
    all_to_all x1, waiting for transfers between devices, per_device(): lax.all_to_all(pieces, 'tensor', split_axis=0, concat_axis=0, tiled=True)  10.1 us
    all_gather x1, blocking collectives, per_device(): lax.all_gather(kv_rows, 'ctx', axis=0, tiled=True)  8.92 us
    dot_general x1, matrix products, per_device(): lax.dot_general(kv_all, wide_weight, (((0, 2), (0, 2)), ((), ())), prefer...  6.71 us
  transfers between devices with their start and end apart: 8, of which 7 were waited for; matrix products, arithmetic and copies ran while one was open for 17% of the time, Pallas kernels for 0%

profile of v1, /device:TPU:0, one launch (start us, length us, event | category | flops | bytes accessed | tf_op | source)
XLA Modules:
  0.0 305.0 jit_solution(4992728812437884992)
XLA Ops:
  7.2 0.7 all-gather.6.cloned.1.call-update
  8.0 0.7 fusion.18
  8.7 0.7 bitcast_multiply_fusion.1
  9.4 1.2 gather_fusion
  10.6 0.7 compare_and_fusion.1
  11.4 0.1 copy.45
  11.5 0.6 gather_fusion.2
  12.1 0.7 compare_and_fusion
  12.8 0.1 copy.46
  12.9 0.7 bitcast_multiply_fusion
  13.8 1.9 gather_fusion.1
  15.8 3.5 %gather_fusion.3 = s32[512]{0:T(512)S(1)} fusion(s32[512]{0:T(512)S(1)} %bitcast.162, s32[1024]{0:T(1024)S(1)} %get-tuple-element.106), kind=kCustom, calls=%fused_computation.1.clone | custom fusion | bytes 6144 | tf_op jit(solution)/shard_map/while/body/eval_jaxpr/jit(_take)/gather | solution.py:71
  19.5 0.1 broadcast_in_dim.108
  19.7 0.2 fusion.17
  19.9 0.3 copy.47
  20.2 0.5 copy.77
  20.7 1.5 copy.79
  22.2 1.6 copy.57
  23.8 0.2 convert_bitcast_fusion
  24.0 0.4 copy.80
  24.4 0.9 multiply_reduce_fusion
  25.3 0.1 copy.52
  25.4 67.7 %all-gather.6.cloned.1.call-done = bf16[1,256,8192]{2,1,0:T(8,128)(2,1)} async-done(((bf16[1,64,8192]{2,1,0:T(8,128)(2,1)}), bf16[1,256,8192]{2,1,0:T(8,128)(2,1)}) %all-gather.6.cloned.1.call-update) | async-done | bytes 4194320 | tf_op jit(solution)/shard_map/all_gather | solution.py:28
  93.1 5.3 %convolution_convert_fusion.1 = bf16[256,256]{0,1:T(8,128)(2,1)S(1)} fusion(bf16[8192,256]{1,0:T(8,128)(2,1)} %param.18, bf16[1,256,8192]{2,1,0:T(8,128)(2,1)} %all-gather.6.cloned.1.call-done), kind=kOutput, calls=%fused_computation.22 | convolution fusion | flops 1073807360 | bytes 8519680 | tf_op jit(solution)/shard_map/dot_general | solution.py:46
  98.4 0.6 copy-done.5
  99.0 1.9 convolution_convert_fusion.2
  100.9 8.9 %all_gather.20 = bf16[512,512]{0,1:T(8,128)(2,1)S(1)} all-gather(bf16[256,512]{0,1:T(8,128)(2,1)S(1)} %pad_maximum_fusion.2), channel_id=1, replica_groups=mesh['dp'=4,'ctx'=2,'tensor'=4] {'ctx'}, dimensions={0}, use_global_device_ids=true | all-gather | bytes 786432 | tf_op jit(solution)/shard_map/all_gather | solution.py:169
  109.9 1.4 fusion.3
  111.3 1.7 exponential_reduce_fusion
  113.0 2.3 fusion.4
  115.3 2.9 fusion.1
  118.2 2.0 copy-done.4
  120.2 1.5 fusion.8
  121.7 1.0 pad_maximum_fusion
  122.7 1.3 dynamic-slice_bitcast_fusion
  124.0 1.1 pad_maximum_fusion.1
  125.1 3.6 %all-to-all-start = ((bf16[4,256,512]{2,1,0:T(8,128)(2,1)}), bf16[4,256,512]{2,1,0:T(8,128)(2,1)S(1)}, u32[]{:S(2)}, u32[]{:S(2)}) async-start(bf16[4,256,512]{2,1,0:T(8,128)(2,1)} %pad_maximum_fusion.1), calls=%async_computation.1 | async-start | bytes 2097152 | tf_op jit(solution)/shard_map/all_to_all | solution.py:40
  128.7 13.1 %reduce-scatter.2.cloned.1.call-done = f32[256,512]{0,1:T(8,128)} async-done(((f32[512,512]{0,1:T(8,128)}), f32[256,512]{0,1:T(8,128)}) %reduce-scatter.2.cloned.1.call-update) | async-done | bytes 524304 | tf_op jit(solution)/shard_map/reduce_scatter | solution.py:171
  141.8 1.8 convert_element_type.47
  143.7 10.1 %all-to-all-done = bf16[4,256,512]{2,1,0:T(8,128)(2,1)S(1)} async-done(((bf16[4,256,512]{2,1,0:T(8,128)(2,1)}), bf16[4,256,512]{2,1,0:T(8,128)(2,1)S(1)}, u32[]{:S(2)}, u32[]{:S(2)}) %all-to-all-start) | async-done | bytes 1048608 | tf_op jit(solution)/shard_map/all_to_all | solution.py:40
  153.7 1.0 copy-done.6
  154.7 2.0 fusion.16
  156.8 1.9 fusion.15
  158.7 1.9 fusion.14
  160.5 1.9 fusion.13
  162.4 0.9 fusion.12
  163.3 0.9 fusion.11
  164.1 0.9 fusion.10
  165.0 0.8 fusion.9
  165.8 4.6 %all-to-all-start.2 = ((bf16[8,256,1024]{2,1,0:T(8,128)(2,1)}), bf16[8,256,1024]{2,1,0:T(8,128)(2,1)}, u32[]{:S(2)}, u32[]{:S(2)}) async-start(bf16[8,256,1024]{2,1,0:T(8,128)(2,1)} %fusion.9), calls=%async_computation.3 | async-start | bytes 8388608 | tf_op jit(solution)/shard_map/all_to_all | solution.py:43
  170.5 0.5 all-gather.10.cloned.1.call-update
  171.0 3.3 %all-gather.12.cloned.1.call-done = bf16[1024,512]{0,1:T(8,128)(2,1)} async-done(((bf16[256,512]{0,1:T(8,128)(2,1)}), bf16[1024,512]{0,1:T(8,128)(2,1)}) %all-gather.12.cloned.1.call-update) | async-done | bytes 1048592 | tf_op jit(solution)/shard_map/all_gather | solution.py:177
  174.3 1.5 copy.58
  175.8 82.8 %all-gather.8.cloned.1.call-done = bf16[4,2048,512]{2,1,0:T(8,128)(2,1)} async-done(((bf16[4,256,512]{2,1,0:T(8,128)(2,1)}), bf16[4,2048,512]{2,1,0:T(8,128)(2,1)}) %all-gather.8.cloned.1.call-update) | async-done | bytes 8388624 | tf_op jit(solution)/shard_map/all_gather | solution.py:41
  258.6 6.7 %fusion.7 = bf16[256,2048]{1,0:T(8,128)(2,1)} fusion(bf16[4,256,512]{2,1,0:T(8,128)(2,1)S(1)} %bitcast.185, bf16[4,2048,512]{2,1,0:T(8,128)(2,1)} %all-gather.8.cloned.1.call-done), kind=kOutput, calls=%fused_computation.15 | convolution fusion | flops 2148007936 | bytes 10485760 | tf_op jit(solution)/shard_map/dot_general | solution.py:179
  265.3 4.6 %all-to-all-start.1 = ((bf16[4,64,2048]{2,1,0:T(8,128)(2,1)}), bf16[4,64,2048]{2,1,0:T(8,128)(2,1)S(1)}, u32[]{:S(2)}, u32[]{:S(2)}) async-start(bf16[4,64,2048]{2,1,0:T(8,128)(2,1)} %bitcast.37), calls=%async_computation.2 | async-start | bytes 2097152 | tf_op jit(solution)/shard_map/all_to_all | solution.py:182
  269.9 2.9 multiply_convert_fusion
  272.8 1.4 copy.62
  274.2 15.0 %all-gather.10.cloned.1.call-done = bf16[2048,512]{0,1:T(8,128)(2,1)} async-done(((bf16[256,512]{0,1:T(8,128)(2,1)}), bf16[2048,512]{0,1:T(8,128)(2,1)}) %all-gather.10.cloned.1.call-update) | async-done | bytes 2097168 | tf_op jit(solution)/shard_map/all_gather | solution.py:178
  289.3 5.3 %convolution_convert_fusion = bf16[1024,512]{1,0:T(8,128)(2,1)S(1)} fusion(bf16[2048,1024]{1,0:T(8,128)(2,1)} %bitcast.47, bf16[2048,512]{0,1:T(8,128)(2,1)} %all-gather.10.cloned.1.call-done), kind=kOutput, calls=%fused_computation.19 | convolution fusion | flops 2148007936 | bytes 7340032 | tf_op jit(solution)/shard_map/dot_general | solution.py:183
  294.5 1.0 fusion.24
  295.6 0.5 all-to-all-done.1
  296.1 0.8 copy.61
  296.9 1.6 broadcast_in_dim.114
  (40 shorter events, 0.9 us)
Async XLA Ops:
  7.2 6.7 %copy-start = (s32[1,512]{1,0:T(1,128)S(1)}, s32[1,512]{1,0:T(1,128)}, u32[]{:S(2)}) copy-start(s32[1,512]{1,0:T(1,128)} %param.19) | copy-start | bytes 6148
  7.2 13.0 %copy-start.8 = (bf16[1,256,2048]{2,1,0:T(8,128)(2,1)S(1)}, bf16[1,256,2048]{2,1,0:T(8,128)(2,1)}, u32[]{:S(2)}) copy-start(bf16[1,256,2048]{2,1,0:T(8,128)(2,1)} %param.14) | copy-start | bytes 3145732
  7.2 85.9 %all-gather.6.cloned.1.call-start = ((), (), s32[]{:S(2)}) async-start(), calls=%async_computation.4 | async-start | bytes 5242880 | tf_op jit(solution)/shard_map/all_gather | solution.py:28
  7.9 133.9 %reduce-scatter.2.cloned.1.call-start = ((), (), s32[]{:S(2)}) async-start(), calls=%async_computation.5 | async-start | bytes 1572864 | tf_op jit(solution)/shard_map/reduce_scatter | solution.py:171
  15.8 8.0 %copy-start.7 = (bf16[1,256,2048]{2,1,0:T(8,128)(2,1)S(1)}, bf16[1,256,2048]{2,1,0:T(8,128)(2,1)}, u32[]{:S(2)}) copy-start(bf16[1,256,2048]{2,1,0:T(8,128)(2,1)} %param.15) | copy-start | bytes 3145732
  93.1 5.3 %copy-start.2 = (bf16[1,256,8192]{2,1,0:T(8,128)(2,1)S(1)}, bf16[1,256,8192]{2,1,0:T(8,128)(2,1)}, u32[]{:S(2)}) copy-start(bf16[1,256,8192]{2,1,0:T(8,128)(2,1)} %all-gather.6.cloned.1.call-done) | copy-start | bytes 12582916
  93.1 5.9 %copy-start.5 = (bf16[8192,256]{1,0:T(8,128)(2,1)S(1)}, bf16[8192,256]{1,0:T(8,128)(2,1)}, u32[]{:S(2)}) copy-start(bf16[8192,256]{1,0:T(8,128)(2,1)} %param.17) | copy-start | bytes 12582916
  111.3 1.8 copy-start.9
  118.2 2.0 copy-start.4
  125.1 28.6 %all-to-all-start = ((bf16[4,256,512]{2,1,0:T(8,128)(2,1)}), bf16[4,256,512]{2,1,0:T(8,128)(2,1)S(1)}, u32[]{:S(2)}, u32[]{:S(2)}) async-start(bf16[4,256,512]{2,1,0:T(8,128)(2,1)} %pad_maximum_fusion.1), calls=%async_computation.1 | async-start | bytes 2097152 | tf_op jit(solution)/shard_map/all_to_all | solution.py:40
  128.7 45.6 %all-gather.12.cloned.1.call-start = ((), (), s32[]{:S(2)}) async-start(), calls=%async_computation.8 | async-start | bytes 1310720 | tf_op jit(solution)/shard_map/all_gather | solution.py:177
  143.6 115.0 %all-gather.8.cloned.1.call-start = ((), (), s32[]{:S(2)}) async-start(), calls=%async_computation.6 | async-start | bytes 9437184 | tf_op jit(solution)/shard_map/all_gather | solution.py:41
  153.7 1.0 copy-start.6
  154.7 7.7 %copy-start.3 = (bf16[1,256,8192]{2,1,0:T(8,128)(2,1)S(1)}, bf16[1,256,8192]{2,1,0:T(8,128)(2,1)}, u32[]{:S(2)}) copy-start(bf16[1,256,8192]{2,1,0:T(8,128)(2,1)} %all-gather.6.cloned.1.call-done) | copy-start | bytes 12582916
  165.8 99.5 %all-to-all-start.2 = ((bf16[8,256,1024]{2,1,0:T(8,128)(2,1)}), bf16[8,256,1024]{2,1,0:T(8,128)(2,1)}, u32[]{:S(2)}, u32[]{:S(2)}) async-start(bf16[8,256,1024]{2,1,0:T(8,128)(2,1)} %fusion.9), calls=%async_computation.3 | async-start | bytes 8388608 | tf_op jit(solution)/shard_map/all_to_all | solution.py:43
  170.4 118.9 %all-gather.10.cloned.1.call-start = ((), (), s32[]{:S(2)}) async-start(), calls=%async_computation.7 | async-start | bytes 2359296 | tf_op jit(solution)/shard_map/all_gather | solution.py:178
  265.3 30.8 %all-to-all-start.1 = ((bf16[4,64,2048]{2,1,0:T(8,128)(2,1)}), bf16[4,64,2048]{2,1,0:T(8,128)(2,1)S(1)}, u32[]{:S(2)}, u32[]{:S(2)}) async-start(bf16[4,64,2048]{2,1,0:T(8,128)(2,1)} %bitcast.37), calls=%async_computation.2 | async-start | bytes 2097152 | tf_op jit(solution)/shard_map/all_to_all | solution.py:182
  289.3 9.2 %copy-start.1 = (s32[1,512]{1,0:T(1,128)S(1)}, s32[1,512]{1,0:T(1,128)}, u32[]{:S(2)}) copy-start(s32[1,512]{1,0:T(1,128)} %param.19) | copy-start | bytes 6148
Sparse Core Ops, SparseCore 0:
  9.6 83.4 all-gather.5
  122.9 18.9 reduce-scatter.1
  144.0 30.1 all-gather.11
  176.8 81.7 all-gather.7
  261.0 28.1 all-gather.9
